TPU v7x, 32 devices: a whole 2x2x4 slice. The times are simulated.
32 devices in a mesh: dp: 8 (over z, y), tensor: 4 (over x, core).
Axes of the slice: x: 2, y: 2, z: 4, core: 2. Of those that a mesh axis runs over, the one named last changes fastest.
Arguments:
- gradients: bfloat16 [8, 2, 256, 1792], P('dp', None, None, 'tensor'), may hold values from -16 to 16, as said below
- errors: float32 [8, 2, 256, 1792], P('dp', None, None, 'tensor'), may hold values from -4 to 4
- start_factors: float32 [2, 1792, 32], P(None, 'tensor'), may hold values from -5 to 5
- moments: float32 [2, 256, 1792], P(None, 'dp', 'tensor'), may hold values from -2 to 2
- weights: float32 [2, 256, 1792], P(None, 'dp', 'tensor'), may hold values from -5 to 5
- vector_grads: bfloat16 [8, 5, 1792], P('dp', None, 'tensor'), may hold values from -16 to 16, as said below
- vector_moments: float32 [5, 1792], P(None, 'tensor'), may hold values from -2 to 2
- vector_weights: float32 [5, 1792], P(None, 'tensor'), may hold values from 0.5 to 1.5
Outputs:
- new_errors: float32 [8, 2, 256, 1792], P('dp', None, None, 'tensor')
- new_moments: float32 [2, 256, 1792], P(None, 'dp', 'tensor')
- new_weights: bfloat16 [2, 256, 1792], P(None, None, 'tensor')
- new_vector_moments: float32 [5, 1792], P(None, 'tensor')
- new_vector_weights: float32 [5, 1792], P(None, 'tensor')
Inputs may be any that keep to these rules, and one draw needn't show every extreme that they name: `gradients`: each replica's gradient is a part common to all replicas plus its own part. `vector_grads`: each replica's gradient is a part common to all replicas plus its own part.
All inputs are finite; a program needn't handle non-finite values.
Results may differ from a plain program's by a relative error of at most 0.0004.
Values may be sent and summed in bfloat16 or wider, within the bound.
A program may use at most 64 MiB of HBM per device.

v0:
```python
import jax
import jax.numpy as jnp
from jax import lax
from jax.sharding import PartitionSpec as P

ROUNDS = 2
momentum_coef = 0.9
step_rate = 0.1


def basis_from(gram_mat, summed):
    factor_low = jnp.linalg.cholesky(gram_mat)
    return lax.linalg.triangular_solve(
        factor_low, summed, left_side=False, lower=True, transpose_a=True
    )


def left_basis(mixed, right_f):
    partial_value = jnp.einsum("mkd,mdr->mkr", mixed, right_f, precision=lax.Precision.HIGHEST)
    summed = lax.psum(partial_value, ("dp", "tensor"))
    gram_mat = jnp.einsum("mkr,mks->mrs", summed, summed, precision=lax.Precision.HIGHEST)
    return basis_from(gram_mat, summed)


def update(mixed, start, moments, weights):
    right_f = start
    for round_idx in range(ROUNDS):
        basis_now = left_basis(mixed, right_f)
        right_part = jnp.einsum("mkd,mkr->mdr", mixed, basis_now, precision=lax.Precision.HIGHEST)
        right_f = lax.psum(right_part, "dp")
    replicas = lax.axis_size("dp")
    approx = (
        jnp.einsum("mkr,mdr->mkd", basis_now, right_f, precision=lax.Precision.HIGHEST) / replicas
    )
    fresh_errors = mixed - approx
    own_rows = moments.shape[1]
    my_rows = lax.dynamic_slice_in_dim(approx, lax.axis_index("dp") * own_rows, own_rows, 1)
    fresh_moments = momentum_coef * moments + my_rows
    fresh_weights = (weights - step_rate * fresh_moments).astype(jnp.bfloat16)
    regathered = lax.all_gather(fresh_weights, "dp", axis=1, tiled=True)
    return (fresh_errors, fresh_moments, regathered)


def per_device(
    gradients, errors, start_factors, moments, weights, vector_grads, vector_moments, vector_weights
):
    mixed = gradients[0].astype(jnp.float32) + errors[0]
    fresh_errors, fresh_moments, regathered = update(mixed, start_factors, moments, weights)
    vector_total = lax.psum(vector_grads[0].astype(jnp.float32), "dp")
    vector_mean = vector_total / lax.axis_size("dp")
    fresh_vector_moments = momentum_coef * vector_moments + vector_mean
    fresh_vector_weights = vector_weights - step_rate * fresh_vector_moments
    return (
        fresh_errors[None],
        fresh_moments,
        regathered,
        fresh_vector_moments,
        fresh_vector_weights,
    )


def solution(mesh):
    in_specs = (
        P("dp", None, None, "tensor"),
        P("dp", None, None, "tensor"),
        P(None, "tensor", None),
        P(None, "dp", "tensor"),
        P(None, "dp", "tensor"),
        P("dp", None, "tensor"),
        P(None, "tensor"),
        P(None, "tensor"),
    )
    out_specs = (
        P("dp", None, None, "tensor"),
        P(None, "dp", "tensor"),
        P(None, None, "tensor"),
        P(None, "tensor"),
        P(None, "tensor"),
    )
    return jax.shard_map(
        per_device, mesh=mesh, in_specs=in_specs, out_specs=out_specs, check_vma=False
    )
```

profile of v0, /device:TPU:0, one launch (start us, length us, event | category | flops | bytes accessed | tf_op | source)
XLA Modules:
  0.0 471.9 jit_solution(15930844537223940268)
XLA Ops:
  7.2 0.0 copy-start
  7.2 0.0 copy-start.1
  7.2 0.0 all-reduce.5.cloned.1.call-start
  7.2 0.8 copy-done
  8.1 2.6 fusion.6
  10.7 0.0 copy-start.2
  10.7 0.0 all-reduce.5.cloned.1.call-update
  10.7 0.0 all-reduce.7.cloned.1.call-start
  10.8 123.7 %all-reduce.5.cloned.1.call-done = f32[2,256,32]{1,2,0:T(8,128)} async-done(((f32[2,256,32]{1,2,0:T(8,128)}), f32[2,256,32]{1,2,0:T(8,128)}) %all-reduce.5.cloned.1.call-update) | async-done | bytes 65552 | tf_op jit(solution)/shard_map/psum | solution.py:20
  134.5 1.1 fusion.13
  135.6 0.1 copy.27
  135.7 5.9 %custom-call.8 = f32[2,32,32]{2,1,0:T(8,128)S(1)} custom-call(f32[2,32,32]{2,1,0:T(8,128)S(1)} %fusion.12), custom_call_target="Cholesky" | custom-call | tf_op jit(solution)/shard_map/jit(cholesky)/cholesky | solution.py:12
  141.6 0.1 compare_reduce_fusion.1
  141.7 0.1 select_bitcast_fusion.1
  141.8 4.9 %custom-call.9 = f32[2,1,32,32]{2,3,1,0:T(8,128)S(1)} custom-call(f32[2,1,32,32]{3,2,1,0:T(8,128)S(1)} %select_bitcast_fusion.1), custom_call_target="InvertDiagBlocksLowerTriangular" | custom-call | tf_op jit(solution)/shard_map/triangular_solve/custom-call.0 | solution.py:13
  146.7 1.1 convolution_bitcast_fusion.1
  147.8 0.0 copy-done.1
  147.8 0.0 copy-done.2
  147.8 1.6 fusion.4
  149.4 0.0 all-reduce.7.cloned.1.call-update
  149.5 0.0 all-reduce.9.cloned.1.call-start
  149.5 70.5 %all-reduce.7.cloned.1.call-done = f32[2,448,32]{1,2,0:T(8,128)} async-done(((f32[2,448,32]{1,2,0:T(8,128)}), f32[2,448,32]{1,2,0:T(8,128)}) %all-reduce.7.cloned.1.call-update) | async-done | bytes 114704 | tf_op jit(solution)/shard_map/psum | solution.py:30
  220.0 0.0 copy-start.4
  220.0 2.3 fusion.2
  222.3 0.0 copy-start.8
  222.3 0.0 all-reduce.9.cloned.1.call-update
  222.3 0.0 all-reduce.11.cloned.1.call-start
  222.4 0.6 copy-done.8
  223.0 0.0 copy-done.4
  223.0 0.0 copy-start.5
  223.0 0.2 copy.31
  223.2 0.7 copy-done.5
  223.9 0.2 copy.32
  224.1 35.5 %psum.39 = f32[5,448]{1,0:T(8,128)S(1)} all-reduce(f32[5,448]{1,0:T(8,128)S(1)} %bitcast_convert_fusion), channel_id=1, replica_groups=mesh['dp'=8,'tensor'=4] {'dp'}, use_global_device_ids=true, to_apply=%region_6.9 | all-reduce | flops 2240 | bytes 17920 | tf_op jit(solution)/shard_map/psum | solution.py:49
  259.6 84.4 %all-reduce.9.cloned.1.call-done = f32[2,256,32]{1,2,0:T(8,128)} async-done(((f32[2,256,32]{1,2,0:T(8,128)}), f32[2,256,32]{1,2,0:T(8,128)}) %all-reduce.9.cloned.1.call-update) | async-done | bytes 65552 | tf_op jit(solution)/shard_map/psum | solution.py:20
  344.0 1.1 fusion.14
  345.1 0.1 copy.29
  345.1 0.0 copy-start.3
  345.2 5.9 %custom-call.10 = f32[2,32,32]{2,1,0:T(8,128)S(1)} custom-call(f32[2,32,32]{2,1,0:T(8,128)S(1)} %fusion.10), custom_call_target="Cholesky" | custom-call | tf_op jit(solution)/shard_map/jit(cholesky)/cholesky | solution.py:12
  351.1 0.1 compare_reduce_fusion
  351.2 0.1 select_bitcast_fusion
  351.3 4.9 %custom-call.11 = f32[2,1,32,32]{2,3,1,0:T(8,128)S(1)} custom-call(f32[2,1,32,32]{3,2,1,0:T(8,128)S(1)} %select_bitcast_fusion), custom_call_target="InvertDiagBlocksLowerTriangular" | custom-call | tf_op jit(solution)/shard_map/triangular_solve/custom-call.0 | solution.py:13
  356.2 0.0 copy-done.3
  356.2 0.3 convolution_bitcast_fusion
  356.5 1.6 fusion
  358.1 0.0 copy-start.6
  358.1 0.0 copy-start.7
  358.1 0.0 all-reduce.11.cloned.1.call-update
  358.1 0.7 copy-done.6
  358.8 0.0 copy-done.7
  358.8 0.6 multiply_subtract_fusion
  359.4 69.2 %all-reduce.11.cloned.1.call-done = f32[2,448,32]{1,2,0:T(8,128)} async-done(((f32[2,448,32]{1,2,0:T(8,128)}), f32[2,448,32]{1,2,0:T(8,128)}) %all-reduce.11.cloned.1.call-update) | async-done | bytes 114704 | tf_op jit(solution)/shard_map/psum | solution.py:30
  428.7 1.8 convolution_multiply_fusion
  430.5 1.1 fusion.8
  431.6 0.2 subtract_convert_fusion
  431.8 0.1 copy.33
  431.9 0.8 copy.34
  432.8 31.5 %all_gather.3 = bf16[2,256,448]{2,0,1:T(2,128)(2,1)S(1)} all-gather(bf16[2,32,448]{2,0,1:T(2,128)(2,1)S(1)} %copy.33), channel_id=1, replica_groups=mesh['dp'=8,'tensor'=4] {'dp'}, dimensions={1}, use_global_device_ids=true | all-gather | bytes 516096 | tf_op jit(solution)/shard_map/all_gather | solution.py:40
  464.3 1.1 copy.35
  (7 shorter events, 0.1 us)
Async XLA Ops:
  7.2 0.9 copy-start
  7.2 140.6 %copy-start.1 = (f32[1,2,256,448]{2,3,1,0:T(8,128)S(1)}, f32[1,2,256,448]{2,3,1,0:T(8,128)}, u32[]{:S(2)}) copy-start(f32[1,2,256,448]{2,3,1,0:T(8,128)} %param.12) | copy-start | bytes 2752516
  7.2 127.3 %all-reduce.5.cloned.1.call-start = ((), (), s32[]{:S(2)}) async-start(), calls=%async_computation | async-start | bytes 131072 | tf_op jit(solution)/shard_map/psum | solution.py:20
  10.7 137.1 %copy-start.2 = (bf16[1,2,256,448]{2,3,1,0:T(8,128)(2,1)S(1)}, bf16[1,2,256,448]{2,3,1,0:T(8,128)(2,1)}, u32[]{:S(2)}) copy-start(bf16[1,2,256,448]{2,3,1,0:T(8,128)(2,1)} %param.11) | copy-start | bytes 1376260
  10.7 209.3 %all-reduce.7.cloned.1.call-start = ((), (), s32[]{:S(2)}) async-start(), calls=%async_computation.1 | async-start | bytes 262144 | tf_op jit(solution)/shard_map/psum | solution.py:30
  149.5 194.5 %all-reduce.9.cloned.1.call-start = ((), (), s32[]{:S(2)}) async-start(), calls=%async_computation.2 | async-start | bytes 131072 | tf_op jit(solution)/shard_map/psum | solution.py:20
  220.0 3.0 copy-start.4
  222.3 0.7 copy-start.8
  222.3 206.3 %all-reduce.11.cloned.1.call-start = ((), (), s32[]{:S(2)}) async-start(), calls=%async_computation.3 | async-start | bytes 262144 | tf_op jit(solution)/shard_map/psum | solution.py:30
  223.0 0.9 copy-start.5
  345.1 11.0 %copy-start.3 = (f32[2,256,32]{1,2,0:T(8,128)S(1)}, f32[2,256,32]{1,2,0:T(8,128)}, u32[]{:S(2)}) copy-start(f32[2,256,32]{1,2,0:T(8,128)} %all-reduce.9.cloned.1.call-done) | copy-start | bytes 196612
  358.1 0.7 copy-start.6
  358.1 0.7 copy-start.7
Sparse Core Ops, SparseCore 0:
  14.2 120.2 all-reduce.4
  149.6 70.3 all-reduce.6
  227.1 116.7 all-reduce.8
  358.2 70.3 all-reduce.10
where the time goes:
time: 472 us
  waiting for transfers between devices  348 us (74%)
  blocking collectives  67 us (14%)
  other arithmetic  23.9 us (5%)
  between operations  13.9 us (3%)
  matrix products  13.6 us (3%)
  local copies, waits for them, and re-layouts  5.47 us (1%)
    psum x2, waiting for transfers between devices, left_basis(): summed = lax.psum(partial_value, ('dp', 'tensor'))  208 us
    psum x2, waiting for transfers between devices, update(): right_f = lax.psum(right_part, 'dp')  140 us
    psum x1, blocking collectives, per_device(): vector_total = lax.psum(vector_grads[0].astype(jnp.float32), 'dp')  35.5 us
    all_gather x1, blocking collectives, update(): regathered = lax.all_gather(fresh_weights, 'dp', axis=1, tiled=True)  31.5 us
    another operation x7, other arithmetic, basis_from(): factor_low = jnp.linalg.cholesky(gram_mat)  12 us
    another operation x5, other arithmetic, basis_from(): lax.linalg.triangular_solve(factor_low, summed, left_side=False, lower=Tr...  9.99 us
  transfers between devices with their start and end apart: 4, of which 4 were waited for; matrix products, arithmetic and copies ran while one was open for 0% of the time, Pallas kernels for 0%

commit v1 on v0

--- a/solution.py
+++ b/solution.py
@@ -6,6 +6,23 @@
 ROUNDS = 2
 momentum_coef = 0.9
 step_rate = 0.1
+
+
+def in_order(parts, dim):
+    parts = jnp.moveaxis(parts, 0, dim)
+    shape = parts.shape
+    return parts.reshape(*shape[:dim], shape[dim] * shape[dim + 1], *shape[dim + 2 :])
+
+
+def doubled(shard, axis):
+    length, index = (lax.axis_size(axis), lax.axis_index(axis))
+    blocks, bit = (shard[None], 1)
+    while bit < length:
+        other = lax.ppermute(blocks, axis, [(i, i ^ bit) for i in range(length)])
+        low = index & bit == 0
+        blocks = jnp.concatenate([jnp.where(low, blocks, other), jnp.where(low, other, blocks)])
+        bit *= 2
+    return blocks
 
 
 def basis_from(gram_mat, summed):
@@ -37,7 +54,7 @@
     my_rows = lax.dynamic_slice_in_dim(approx, lax.axis_index("dp") * own_rows, own_rows, 1)
     fresh_moments = momentum_coef * moments + my_rows
     fresh_weights = (weights - step_rate * fresh_moments).astype(jnp.bfloat16)
-    regathered = lax.all_gather(fresh_weights, "dp", axis=1, tiled=True)
+    regathered = in_order(doubled(fresh_weights, "dp"), 1)
     return (fresh_errors, fresh_moments, regathered)
 
 

time: 472 us -> 493 us (1.044)
  waiting for transfers between devices: 348 us -> 395 us
  blocking collectives: 67 us -> 36 us
    psum x2, waiting for transfers between devices: 208 us -> 245 us  [left_basis(): summed = lax.psum(partial_value, ('dp', 'tensor'))]
    all_gather x1 -> x0, blocking collectives: 31.5 us -> none  [update(): regathered = lax.all_gather(fresh_weights, 'dp', axis=1, tiled=True)]
    ppermute x0 -> x3, waiting for transfers between devices: none -> 11.3 us  [doubled(): other = lax.ppermute(blocks, axis, [(i, i ^ bit) for i in range(length)])]
  transfers between devices with their start and end apart: 4 -> 7, of which waited for: 4 -> 6; matrix products, arithmetic and copies ran while one was open for 0% -> 1% of each run, Pallas kernels for 0% -> 0%
where the time goes in v1:
time: 493 us; the launch traced here: 492 us
  waiting for transfers between devices  395 us (80%)
  blocking collectives  36 us (7%)
  other arithmetic  25.9 us (5%)
  between operations  14 us (3%)
  matrix products  13.6 us (3%)
  local copies, waits for them, and re-layouts  6.46 us (1%)
    psum x2, waiting for transfers between devices, left_basis(): summed = lax.psum(partial_value, ('dp', 'tensor'))  245 us
    psum x2, waiting for transfers between devices, update(): right_f = lax.psum(right_part, 'dp')  138 us
    psum x1, blocking collectives, per_device(): vector_total = lax.psum(vector_grads[0].astype(jnp.float32), 'dp')  36 us
    another operation x7, other arithmetic, basis_from(): factor_low = jnp.linalg.cholesky(gram_mat)  12 us
    ppermute x3, waiting for transfers between devices, doubled(): other = lax.ppermute(blocks, axis, [(i, i ^ bit) for i in range(length)])  11.3 us
    another operation x5, other arithmetic, basis_from(): lax.linalg.triangular_solve(factor_low, summed, left_side=False, lower=Tr...  9.99 us
  transfers between devices with their start and end apart: 7, of which 6 were waited for; matrix products, arithmetic and copies ran while one was open for 1% of the time, Pallas kernels for 0%

profile of v1, /device:TPU:0, one launch (start us, length us, event | category | flops | bytes accessed | tf_op | source)
XLA Modules:
  0.0 492.1 jit_solution(14338834570174390373)
XLA Ops:
  7.2 0.0 copy-start
  7.2 0.0 copy-start.1
  7.2 0.0 all-reduce.5.cloned.1.call-start
  7.2 0.8 copy-done
  8.1 2.6 fusion.6
  10.7 0.0 all-reduce.5.cloned.1.call-update
  10.7 0.0 all-reduce.7.cloned.1.call-start
  10.8 123.6 %all-reduce.5.cloned.1.call-done = f32[2,256,32]{1,2,0:T(8,128)} async-done(((f32[2,256,32]{1,2,0:T(8,128)}), f32[2,256,32]{1,2,0:T(8,128)}) %all-reduce.5.cloned.1.call-update) | async-done | bytes 65552 | tf_op jit(solution)/shard_map/psum | solution.py:37
  134.5 1.1 fusion.14
  135.6 0.1 copy.38
  135.6 5.9 %custom-call.8 = f32[2,32,32]{2,1,0:T(8,128)S(1)} custom-call(f32[2,32,32]{2,1,0:T(8,128)S(1)} %fusion.13), custom_call_target="Cholesky" | custom-call | tf_op jit(solution)/shard_map/jit(cholesky)/cholesky | solution.py:29
  141.5 0.1 compare_reduce_fusion.1
  141.7 0.1 select_bitcast_fusion.1
  141.7 4.9 custom-call.9
  146.7 1.1 convolution_bitcast_fusion.1
  147.8 0.0 copy-done.1
  147.8 0.0 copy-done.2
  147.8 1.6 fusion.4
  149.4 0.0 all-reduce.7.cloned.1.call-update
  149.5 0.0 all-reduce.9.cloned.1.call-start
  149.5 70.5 %all-reduce.7.cloned.1.call-done = f32[2,448,32]{1,2,0:T(8,128)} async-done(((f32[2,448,32]{1,2,0:T(8,128)}), f32[2,448,32]{1,2,0:T(8,128)}) %all-reduce.7.cloned.1.call-update) | async-done | bytes 114704 | tf_op jit(solution)/shard_map/psum | solution.py:47
  220.0 2.2 fusion.2
  222.3 0.0 all-reduce.9.cloned.1.call-update
  222.3 0.0 all-reduce.11.cloned.1.call-start
  222.4 121.6 %all-reduce.9.cloned.1.call-done = f32[2,256,32]{1,2,0:T(8,128)} async-done(((f32[2,256,32]{1,2,0:T(8,128)}), f32[2,256,32]{1,2,0:T(8,128)}) %all-reduce.9.cloned.1.call-update) | async-done | bytes 65552 | tf_op jit(solution)/shard_map/psum | solution.py:37
  344.0 1.1 fusion.15
  345.1 0.1 copy.40
  345.2 5.9 %custom-call.10 = f32[2,32,32]{2,1,0:T(8,128)S(1)} custom-call(f32[2,32,32]{2,1,0:T(8,128)S(1)} %fusion.11), custom_call_target="Cholesky" | custom-call | tf_op jit(solution)/shard_map/jit(cholesky)/cholesky | solution.py:29
  351.1 0.1 compare_reduce_fusion
  351.2 0.1 select_bitcast_fusion
  351.3 4.9 custom-call.11
  356.2 0.3 convolution_bitcast_fusion
  356.5 1.6 fusion
  358.1 0.0 all-reduce.11.cloned.1.call-update
  358.1 0.9 copy-done.5
  359.0 0.2 copy.42
  359.2 0.7 copy-done.6
  359.9 1.0 copy.43
  360.9 67.8 %all-reduce.11.cloned.1.call-done = f32[2,448,32]{1,2,0:T(8,128)} async-done(((f32[2,448,32]{1,2,0:T(8,128)}), f32[2,448,32]{1,2,0:T(8,128)}) %all-reduce.11.cloned.1.call-update) | async-done | bytes 114704 | tf_op jit(solution)/shard_map/psum | solution.py:47
  428.7 1.9 convolution_multiply_fusion
  430.6 0.0 copy-done.3
  430.6 0.0 copy-start.9
  430.6 0.9 fusion.9
  431.5 0.8 collective-permute-start
  432.3 0.0 copy-done.9
  432.3 36.0 %psum.39 = f32[5,448]{1,0:T(8,128)S(1)} all-reduce(f32[5,448]{1,0:T(8,128)S(1)} %bitcast_convert_fusion), channel_id=1, replica_groups=mesh['dp'=8,'tensor'=4] {'dp'}, use_global_device_ids=true, to_apply=%region_6.9 | all-reduce | flops 2240 | bytes 17920 | tf_op jit(solution)/shard_map/psum | solution.py:66
  468.3 0.0 collective-permute-done
  468.3 1.1 broadcast_select_fusion.3
  469.4 0.1 copy.44
  469.5 0.1 copy.45
  469.6 0.0 copy-start.7
  469.6 0.0 copy-start.8
  469.7 0.1 collective-permute-start.1
  469.8 0.6 copy-done.7
  470.4 0.0 copy-done.8
  470.4 0.6 multiply_subtract_fusion
  471.0 0.8 copy.47
  471.8 2.9 collective-permute-done.1
  474.8 0.1 collective-permute-start.2
  474.9 1.1 fusion.8
  475.9 8.4 %collective-permute-done.2 = bf16[4,2,32,448]{3,2,1,0:T(8,128)(2,1)S(1)} collective-permute-done((bf16[4,2,32,448]{3,2,1,0:T(8,128)(2,1)S(1)}, bf16[4,2,32,448]{3,2,1,0:T(8,128)(2,1)S(1)}, u32[]{:S(2)}, u32[]{:S(2)}) %collective-permute-start.2) | collective-permute-done | bytes 229408 | tf_op jit(solution)/shard_map/ppermute | solution.py:21
  484.4 0.1 broadcast_select_fusion.1
  484.4 0.1 maximum_bitcast_fusion
  484.5 1.0 copy.48
  (17 shorter events, 0.2 us)
Async XLA Ops:
  7.2 0.9 copy-start
  7.2 140.6 %copy-start.1 = (f32[1,2,256,448]{2,3,1,0:T(8,128)S(1)}, f32[1,2,256,448]{2,3,1,0:T(8,128)}, u32[]{:S(2)}) copy-start(f32[1,2,256,448]{2,3,1,0:T(8,128)} %param.12) | copy-start | bytes 2752516
  7.2 127.3 %all-reduce.5.cloned.1.call-start = ((), (), s32[]{:S(2)}) async-start(), calls=%async_computation | async-start | bytes 131072 | tf_op jit(solution)/shard_map/psum | solution.py:37
  10.7 137.1 %copy-start.2 = (bf16[1,2,256,448]{2,3,1,0:T(8,128)(2,1)S(1)}, bf16[1,2,256,448]{2,3,1,0:T(8,128)(2,1)}, u32[]{:S(2)}) copy-start(bf16[1,2,256,448]{2,3,1,0:T(8,128)(2,1)} %param.11) | copy-start | bytes 1376260
  10.7 209.3 %all-reduce.7.cloned.1.call-start = ((), (), s32[]{:S(2)}) async-start(), calls=%async_computation.1 | async-start | bytes 262144 | tf_op jit(solution)/shard_map/psum | solution.py:47
  149.5 194.5 %all-reduce.9.cloned.1.call-start = ((), (), s32[]{:S(2)}) async-start(), calls=%async_computation.2 | async-start | bytes 131072 | tf_op jit(solution)/shard_map/psum | solution.py:37
  222.3 206.4 %all-reduce.11.cloned.1.call-start = ((), (), s32[]{:S(2)}) async-start(), calls=%async_computation.3 | async-start | bytes 262144 | tf_op jit(solution)/shard_map/psum | solution.py:47
  345.2 11.0 %copy-start.4 = (f32[2,256,32]{1,2,0:T(8,128)S(1)}, f32[2,256,32]{1,2,0:T(8,128)}, u32[]{:S(2)}) copy-start(f32[2,256,32]{1,2,0:T(8,128)} %all-reduce.9.cloned.1.call-done) | copy-start | bytes 196612
  358.1 0.9 copy-start.5
  359.0 0.9 copy-start.6
  428.7 1.9 copy-start.3
  430.6 1.7 copy-start.9
  431.5 36.8 %collective-permute-start = (bf16[1,2,32,448]{2,3,1,0:T(8,128)(2,1)}, bf16[1,2,32,448]{2,3,1,0:T(8,128)(2,1)}, u32[]{:S(2)}, u32[]{:S(2)}) collective-permute-start(bf16[1,2,32,448]{2,3,1,0:T(8,128)(2,1)} %get-tuple-element.29), channel_id=1, source_target_pairs={{0,4},{4,0},{8,12},{12,8},{16,20},{20,16},{24,28},{28,24},{1,5},{5... | collective-permute-start | bytes 172040 | tf_op jit(solution)/shard_map/ppermute | solution.py:21
  469.6 0.7 copy-start.7
  469.6 0.7 copy-start.8
  469.7 5.0 %collective-permute-start.1 = (bf16[2,2,32,448]{3,2,1,0:T(8,128)(2,1)S(1)}, bf16[2,2,32,448]{3,2,1,0:T(8,128)(2,1)S(1)}, u32[]{:S(2)}, u32[]{:S(2)}) collective-permute-start(bf16[2,2,32,448]{3,2,1,0:T(8,128)(2,1)S(1)} %pad_maximum_fusion.1), channel_id=1, source_target_pairs={{0,8},{4,12},{8,0},{12,4},{16,24},{20,28},{24,16},{28,20},{1,9},{5... | collective-permute-start | bytes 344072 | tf_op jit(solution)/shard_map/ppermute | solution.py:21
  474.8 9.6 %collective-permute-start.2 = (bf16[4,2,32,448]{3,2,1,0:T(8,128)(2,1)S(1)}, bf16[4,2,32,448]{3,2,1,0:T(8,128)(2,1)S(1)}, u32[]{:S(2)}, u32[]{:S(2)}) collective-permute-start(bf16[4,2,32,448]{3,2,1,0:T(8,128)(2,1)S(1)} %pad_maximum_fusion), channel_id=1, source_target_pairs={{0,16},{4,20},{8,24},{12,28},{16,0},{20,4},{24,8},{28,12},{1,17},{... | collective-permute-start | bytes 688136 | tf_op jit(solution)/shard_map/ppermute | solution.py:21
Sparse Core Ops, SparseCore 0:
  14.2 120.2 all-reduce.4
  149.6 70.4 all-reduce.6
  227.1 116.7 all-reduce.8
  358.2 70.4 all-reduce.10
